TPU v7x, 32 devices: a whole 2x2x4 slice. The times are simulated.
32 devices in a mesh: grp: 2 (over y), seq: 4 (over z), outer: 4 (over x, core).
Axes of the slice: x: 2, y: 2, z: 4, core: 2. Of those that a mesh axis runs over, the one named last changes fastest.
Arguments:
- inputs: bfloat16 [32768, 512], P(('grp', 'outer', 'seq')), parts along dimension 0, may hold values from -6 to 6
- grad_out: bfloat16 [32768, 512], P(('grp', 'outer', 'seq')), parts along dimension 0, may hold values from -6 to 6
- w_query: bfloat16 [512, 512], replicated, may hold values from -0.25 to 0.25
- w_key: bfloat16 [512, 512], replicated, may hold values from -0.25 to 0.25
- w_value: bfloat16 [512, 512], replicated, may hold values from -0.25 to 0.25
- conv_taps: bfloat16 [4, 512], replicated, may hold values from -3 to 3
Outputs:
- grad_inputs: bfloat16 [32768, 512], P(('grp', 'outer', 'seq')), parts along dimension 0
- grad_wq: float32 [1024, 512], P('grp'), parts along dimension 0
- grad_wk: float32 [1024, 512], P('grp'), parts along dimension 0
- grad_wv: float32 [1024, 512], P('grp'), parts along dimension 0
- grad_conv: float32 [8, 512], P('grp'), parts along dimension 0
There are 2 independent parts, one for each index of `grp`. A program takes and returns all parts, laid end to end along the dimension named above; an argument that names none is the same for every part. Nothing has to cross between parts.
All inputs are finite; a program needn't handle non-finite values.
Results may differ from a plain program's by a relative error of at most 0.0095.
Values may be sent and summed in bfloat16 or wider, within the bound.
A program may use at most 128 MiB of HBM per device.

v0:
```python
import math
import jax
import jax.numpy as jnp
from jax import lax
from jax.sharding import PartitionSpec as P

D = 512
HEADS = 8
HEAD_DIM = 64
TAPS = 4
BLOCK = 512


def shifted(x, axis, by):
    devices = lax.axis_size(axis)
    return lax.ppermute(x, axis, [(i, (i + by) % devices) for i in range(devices)])


def from_behind(value, axis, steps):
    count = lax.axis_size(axis)
    leading, last = (max(0, -steps), min(count, count - steps))
    return lax.ppermute(value, axis, [(source, source + steps) for source in range(leading, last)])


def entering(x, axis, join, neutral, backward):
    count = lax.axis_size(axis)
    place = lax.axis_index(axis)
    ahead = count - 1 - place if backward else place
    gathered = lax.all_gather(x.astype(jnp.bfloat16), axis)
    state = jnp.zeros_like(x) + jnp.asarray(neutral, x.dtype)

    def one(step, state):
        source = count - 1 - step if backward else step
        return join(state, lax.dynamic_index_in_dim(gathered, source, 0, False).astype(x.dtype))

    return lax.fori_loop(0, ahead, one, state)


def add_states(earlier, later):
    return earlier + later


def block_grads(parts):
    queries, key_rows, value_rows, grad_rows, scales, state_prev, state_next = parts
    size = queries.shape[0]
    highest = lax.Precision.HIGHEST
    causal = lax.broadcasted_iota(jnp.int32, (size, size), 0) >= lax.broadcasted_iota(
        jnp.int32, (size, size), 1
    )
    scores = jnp.einsum("thj,shj->hts", grad_rows, value_rows, preferred_element_type=jnp.float32)
    probe = jnp.where(causal[None], scores * scales[None, :, None], 0.0).astype(jnp.bfloat16)
    grad_query = jnp.einsum("hts,shi->thi", probe, key_rows, preferred_element_type=jnp.float32)
    grad_query = grad_query + scales[:, None, None] * jnp.einsum(
        "thj,hij->thi", grad_rows.astype(jnp.float32), state_prev, precision=highest
    )
    grad_key = jnp.einsum("hts,thi->shi", probe, queries, preferred_element_type=jnp.float32)
    grad_key = grad_key + jnp.einsum(
        "shj,hij->shi", value_rows.astype(jnp.float32), state_next, precision=highest
    )
    affinity = jnp.einsum("thi,shi->hts", queries, key_rows, preferred_element_type=jnp.float32)
    mixing = jnp.where(causal[None], affinity * scales[None, :, None], 0.0).astype(jnp.bfloat16)
    grad_value = jnp.einsum("hts,thj->shj", mixing, grad_rows, preferred_element_type=jnp.float32)
    grad_value = grad_value + jnp.einsum(
        "shi,hij->shj", key_rows.astype(jnp.float32), state_next, precision=highest
    )
    return (
        grad_query.reshape(size, D).astype(jnp.bfloat16),
        grad_key.reshape(size, D).astype(jnp.bfloat16),
        grad_value.reshape(size, D).astype(jnp.bfloat16),
    )


def on_device(inputs, grad_out, w_query, w_key, w_value, conv_taps):
    length = inputs.shape[0]
    model_width = inputs.shape[1]
    highest = lax.Precision.HIGHEST
    seq_count = lax.axis_size("seq")
    seq_place = lax.axis_index("seq")
    outer_place = lax.axis_index("outer")
    offset = (outer_place * seq_count + seq_place) * length
    queries = jnp.dot(inputs, w_query, preferred_element_type=jnp.float32).astype(jnp.bfloat16)
    keys_pre = jnp.dot(inputs, w_key, preferred_element_type=jnp.float32).astype(jnp.bfloat16)
    values = jnp.dot(inputs, w_value, preferred_element_type=jnp.float32).astype(jnp.bfloat16)
    tail_rows = keys_pre[length - (TAPS - 1) :]
    wrapped = shifted(tail_rows, "seq", 1)
    across = from_behind(wrapped, "outer", 1)
    before = jnp.where(seq_place == 0, across, wrapped)
    taps = conv_taps.astype(jnp.float32)
    padded = jnp.concatenate([before, keys_pre], 0).astype(jnp.float32)
    keys = jnp.zeros((length, model_width), jnp.float32)
    for tap_index in range(TAPS):
        keys = keys + taps[tap_index] * padded[TAPS - 1 - tap_index : TAPS - 1 - tap_index + length]
    keys = keys.astype(jnp.bfloat16)
    position = (offset + jnp.arange(length, dtype=jnp.int32)).astype(jnp.float32)
    scales = 1.0 / (jnp.sqrt(position + 1.0) * math.sqrt(HEAD_DIM))
    block_count = length // BLOCK
    shape = (block_count, BLOCK, HEADS, HEAD_DIM)
    query_heads = queries.reshape(shape)
    key_heads = keys.reshape(shape)
    value_heads = values.reshape(shape)
    grad_heads = grad_out.reshape(shape)
    block_scales = scales.reshape(block_count, BLOCK)
    kv_blocks = jnp.einsum(
        "nbhi,nbhj->nhij", key_heads, value_heads, preferred_element_type=jnp.float32
    )
    scaled_queries = query_heads.astype(jnp.float32) * block_scales[:, :, None, None]
    qdo_blocks = jnp.einsum(
        "nbhi,nbhj->nhij", scaled_queries, grad_heads.astype(jnp.float32), precision=highest
    )
    kv_local = jnp.sum(kv_blocks, 0)
    qdo_local = jnp.sum(qdo_blocks, 0)
    zeros = jnp.zeros_like(kv_local)
    kv_inner = entering(kv_local, "seq", add_states, zeros, False)
    kv_group, qdo_group = lax.psum((kv_local, qdo_local), "seq")
    kv_outer = entering(kv_group, "outer", add_states, zeros, False)
    qdo_inner = entering(qdo_local, "seq", add_states, zeros, True)
    qdo_outer = entering(qdo_group, "outer", add_states, zeros, True)
    state_before = kv_outer + kv_inner
    state_after = qdo_outer + qdo_inner
    state_prev = state_before[None] + jnp.cumsum(kv_blocks, 0) - kv_blocks
    state_next = state_after[None] + qdo_local[None] - jnp.cumsum(qdo_blocks, 0)
    grad_query, grad_key, grad_value = lax.map(
        block_grads,
        (query_heads, key_heads, value_heads, grad_heads, block_scales, state_prev, state_next),
    )
    grad_query = grad_query.reshape(length, model_width)
    grad_key = grad_key.reshape(length, model_width)
    grad_value = grad_value.reshape(length, model_width)
    head_rows = grad_key[: TAPS - 1]
    wrapped_back = shifted(head_rows, "seq", -1)
    across_back = from_behind(wrapped_back, "outer", -1)
    behind = jnp.where(seq_place == seq_count - 1, across_back, wrapped_back)
    key_grad32 = grad_key.astype(jnp.float32)
    extended = jnp.concatenate([grad_key, behind], 0).astype(jnp.float32)
    grad_pre = jnp.zeros((length, model_width), jnp.float32)
    tap_grads = []
    for tap_index in range(TAPS):
        grad_pre = grad_pre + taps[tap_index] * extended[tap_index : tap_index + length]
        tap_grads.append(
            jnp.sum(key_grad32 * padded[TAPS - 1 - tap_index : TAPS - 1 - tap_index + length], 0)
        )
    grad_pre = grad_pre.astype(jnp.bfloat16)
    conv_local = jnp.stack(tap_grads, 0)
    contract = (((1,), (1,)), ((), ()))
    grad_inputs = lax.dot_general(grad_query, w_query, contract, preferred_element_type=jnp.float32)
    grad_inputs = grad_inputs + lax.dot_general(
        grad_pre, w_key, contract, preferred_element_type=jnp.float32
    )
    grad_inputs = grad_inputs + lax.dot_general(
        grad_value, w_value, contract, preferred_element_type=jnp.float32
    )
    grad_inputs = grad_inputs.astype(jnp.bfloat16)
    over_rows = (((0,), (0,)), ((), ()))
    local_wq = lax.dot_general(inputs, grad_query, over_rows, preferred_element_type=jnp.float32)
    local_wk = lax.dot_general(inputs, grad_pre, over_rows, preferred_element_type=jnp.float32)
    local_wv = lax.dot_general(inputs, grad_value, over_rows, preferred_element_type=jnp.float32)
    grad_wq, grad_wk, grad_wv, grad_conv = lax.psum(
        (local_wq, local_wk, local_wv, conv_local), ("seq", "outer")
    )
    return (grad_inputs, grad_wq, grad_wk, grad_wv, grad_conv)


def solution(mesh):
    in_specs = (
        P(("grp", "outer", "seq"), None),
        P(("grp", "outer", "seq"), None),
        P(),
        P(),
        P(),
        P(),
    )
    out_specs = (
        P(("grp", "outer", "seq"), None),
        P("grp", None),
        P("grp", None),
        P("grp", None),
        P("grp", None),
    )
    return jax.shard_map(
        on_device, mesh=mesh, in_specs=in_specs, out_specs=out_specs, check_vma=False
    )
```

profile of v0, /device:TPU:0, one launch (start us, length us, event | category | flops | bytes accessed | tf_op | source)
XLA Modules:
  0.0 333.5 jit_solution(12223095739537456281)
XLA Ops:
  8.4 1.7 convolution_convert_fusion.2
  11.1 3.0 collective-permute-start
  14.1 2.1 reshape.136
  16.2 2.5 copy.51
  18.8 2.1 convolution_convert_fusion
  20.9 1.3 copy.47
  22.2 1.8 reshape.123
  24.3 2.1 fusion.64
  26.5 15.4 %all-gather.3 = bf16[32,64,64]{2,1,0:T(8,128)(2,1)S(1)} all-gather(bf16[8,64,64]{2,1,0:T(8,128)(2,1)S(1)} %convert_element_type.173), channel_id=5, replica_groups=mesh['grp'=2,'seq'=4,'outer'=4] {'seq'}, dimensions={0}, use_global_device_ids=true | all-gather | bytes 327680 | tf_op jit(solution)/shard_map/all_gather | solution.py:29
  42.2 2.8 convolution_convert_fusion.1
  47.6 2.8 reshape.137
  50.4 2.2 copy.52
  52.6 1.5 maximum_convert_fusion
  54.2 1.9 add_convert_fusion.1
  56.1 3.9 %reshape.135 = bf16[2,512,8,64]{3,2,1,0:T(8,128)(2,1)} reshape(bf16[1024,512]{1,0:T(8,128)(2,1)} %add_convert_fusion.1) | data formatting | bytes 2097152 | tf_op jit(solution)/shard_map/reshape | solution.py:99
  60.0 3.3 copy.50
  63.3 2.8 fusion.63
  66.8 16.7 %all-gather.1 = bf16[32,64,64]{2,1,0:T(8,128)(2,1)} all-gather(bf16[8,64,64]{2,1,0:T(8,128)(2,1)S(1)} %convert_element_type.168), channel_id=3, replica_groups=mesh['grp'=2,'seq'=4,'outer'=4] {'seq'}, dimensions={0}, use_global_device_ids=true | all-gather | bytes 327680 | tf_op jit(solution)/shard_map/all_gather | solution.py:29
  83.5 29.6 %all-reduce.6 = (bf16[8,64,64]{2,1,0:T(8,128)(2,1)}, bf16[8,64,64]{2,1,0:T(8,128)(2,1)S(1)}) all-reduce(f32[8,64,64]{2,1,0:T(8,128)} %copy-done.16, f32[8,64,64]{2,1,0:T(8,128)S(1)} %get-tuple-element.348), channel_id=1, replica_groups=mesh['grp'=2,'seq'=4,'outer'=4] {'seq'}, use_global_device_ids=true, to_apply=%region_1.2 | all-reduce | flops 65536 | bytes 393216 | tf_op jit(solution)/shard_map/psum | solution.py:114
  113.2 7.2 %all-gather = bf16[32,64,64]{2,1,0:T(8,128)(2,1)} all-gather(bf16[8,64,64]{2,1,0:T(8,128)(2,1)} %get-tuple-element.338), channel_id=2, replica_groups=mesh['grp'=2,'seq'=4,'outer'=4] {'outer'}, dimensions={0}, use_global_device_ids=true | all-gather | bytes 327680 | tf_op jit(solution)/shard_map/all_gather | solution.py:29
  121.1 10.4 %all-gather.2 = bf16[32,64,64]{2,1,0:T(8,128)(2,1)} all-gather(bf16[8,64,64]{2,1,0:T(8,128)(2,1)S(1)} %get-tuple-element.339), channel_id=4, replica_groups=mesh['grp'=2,'seq'=4,'outer'=4] {'outer'}, dimensions={0}, use_global_device_ids=true | all-gather | bytes 327680 | tf_op jit(solution)/shard_map/all_gather | solution.py:29
  132.2 5.1 %while.60 = (s32[]{:T(128)}, f32[8,64,64]{2,1,0:T(8,128)}, s32[]{:T(128)}, bf16[4,8,64,64]{3,2,1,0:T(8,128)(2,1)}, s32[]{:T(128)}, /*index=5*/s32[]{:T(128)}, s32[]{:T(128)}, s32[]{:T(128)}) while((s32[]{:T(128)}, f32[8,64,64]{2,1,0:T(8,128)}, s32[]{:T(128)}, bf16[4,8,64,64]{3,2,1,0:T(8,128)(2,1)}, s32[]{:T(128)}, /*index=5*/s32[]{:T(128)}, ...), condition=%wide.region_10.11_spmd, body=%wide.region_9.10_spmd.sunk | while | flops 65542 | bytes 327823 | solution.py:36
  132.2 1.7 convert_add_fusion.10
  134.0 1.7 convert_add_fusion.10
  135.7 1.7 convert_add_fusion.10
  138.5 2.2 fusion.61
  141.6 59.3 %while.62 = (s32[]{:T(128)}, bf16[2,512,512]{2,1,0:T(8,128)(2,1)}, bf16[2,512,512]{2,1,0:T(8,128)(2,1)}, bf16[2,512,512]{2,1,0:T(8,128)(2,1)}, bf16[2,512,8,64]{...) while((s32[]{:T(128)}, bf16[2,512,512]{2,1,0:T(8,128)(2,1)}, ...), condition=%wide.region_15.16_spmd, body=%wide.region_14.15_spmd.sunk | while | flops 1960837120 | bytes 65027896 | solution.py:122
  141.7 3.0 select_convert_fusion.6
  144.7 1.4 fusion.128
  147.3 1.4 fusion.129
  148.7 2.1 copy.80
  150.8 1.9 constant_dynamic-update-slice_fusion.5
  152.6 4.6 %fusion.130 = f32[8,64,512]{2,1,0:T(8,128)} fusion(f32[512]{0:T(512)S(1)} %bitcast.174, pred[512,512]{1,0:T(8,128)(4,1)S(1)} %iota_compare_fusion.2, bf16[2,512,8,64]{1,3,2,0:T(8,128)(2,1)} %get-tuple-element.648, s32[]{:T(128)S(6)} %copy.116, bf16[2,512,8,64]{1,3,2,0:T(8,128)(2,1)} %get-tuple-element.644, bf16[2,512,8,64]{1,3,2,0:T(8,128)(2,1)} %get-tuple-element.643), kind=kOutput, calls=%fused_computation.6.clone.1 | convolution fusion | flops 543162368 | bytes 2887168 | tf_op jit(solution)/shard_map/while/body/eval_jaxpr/hts,thj->shj/dot_general | solution.py:62
  157.2 2.9 fusion.131
  160.1 2.0 copy.81
  162.2 3.3 fusion.132
  165.5 1.4 fusion.133
  166.9 2.1 copy.82
  169.0 2.2 constant_dynamic-update-slice_fusion.6
  171.3 3.0 select_convert_fusion.6
  174.4 1.4 fusion.128
  176.9 1.4 fusion.129
  178.3 2.1 copy.80
  180.4 1.9 constant_dynamic-update-slice_fusion.5
  182.3 4.6 %fusion.130 = f32[8,64,512]{2,1,0:T(8,128)} fusion(f32[512]{0:T(512)S(1)} %bitcast.174, pred[512,512]{1,0:T(8,128)(4,1)S(1)} %iota_compare_fusion.2, bf16[2,512,8,64]{1,3,2,0:T(8,128)(2,1)} %get-tuple-element.648, s32[]{:T(128)S(6)} %copy.116, bf16[2,512,8,64]{1,3,2,0:T(8,128)(2,1)} %get-tuple-element.644, bf16[2,512,8,64]{1,3,2,0:T(8,128)(2,1)} %get-tuple-element.643), kind=kOutput, calls=%fused_computation.6.clone.1 | convolution fusion | flops 543162368 | bytes 2887168 | tf_op jit(solution)/shard_map/while/body/eval_jaxpr/hts,thj->shj/dot_general | solution.py:62
  186.9 2.9 fusion.131
  189.8 2.0 copy.81
  191.8 3.3 fusion.132
  195.1 1.4 fusion.133
  196.6 2.1 copy.82
  198.7 2.2 constant_dynamic-update-slice_fusion.6
  201.6 5.2 %collective-permute-start.2 = (bf16[3,512]{1,0:T(4,128)(2,1)S(1)}, bf16[3,512]{1,0:T(4,128)(2,1)S(1)}, u32[]{:S(2)}, u32[]{:S(2)}) collective-permute-start(bf16[3,512]{1,0:T(4,128)(2,1)S(1)} %slice.73), channel_id=1, source_target_pairs={{0,12},{4,0},{8,4},{12,8},{1,13},{5,1},{9,5},{13,9},{2,14},{6,2},{... | collective-permute-start | bytes 9224 | tf_op jit(solution)/shard_map/ppermute | solution.py:16
  206.8 3.0 convolution_bitcast_fusion.2
  209.8 1.3 collective-permute-start.3
  211.2 1.7 convolution_bitcast_fusion
  215.4 1.7 convolution_bitcast_fusion.1
  217.2 2.3 fusion.51
  219.5 32.9 %psum.47 = f32[4,512]{1,0:T(4,128)} all-reduce(f32[4,512]{1,0:T(4,128)S(1)} %pad_maximum_fusion), channel_id=1, replica_groups=mesh['grp'=2,'seq'=4,'outer'=4] {'seq','outer'}, use_global_device_ids=true, to_apply=%region_23.24 | all-reduce | flops 2048 | bytes 16384 | tf_op jit(solution)/shard_map/psum | solution.py:157
  252.3 2.1 fusion.65
  255.9 1.7 add_convert_fusion
  257.6 63.7 %all-reduce.5.cloned.1.call-done = (f32[512,512]{0,1:T(8,128)}, f32[512,512]{0,1:T(8,128)}, f32[512,512]{0,1:T(8,128)}) async-done(((f32[512,512]{0,1:T(8,128)}, f32[512,512]{0,1:T(8,128)}, f32[512,512]{0,1:T(8,128)}), (f32[512,512]{0,1:T(8,128)}, f32[512,512]{0,1:T(8,128)}, f32[512,512]{0,1:T(8,128)})) %all-reduce.5.cloned.1.call-update) | async-done | bytes 3145744 | tf_op jit(solution)/shard_map/psum | solution.py:157
  321.4 2.7 copy.57
  324.1 1.3 copy.58
  325.4 1.3 copy.59
  (128 shorter events, 16.9 us)
Async XLA Ops:
  7.2 1.2 copy-start
  7.2 7.0 %copy-start.19 = (bf16[1024,512]{1,0:T(8,128)(2,1)S(1)}, bf16[1024,512]{1,0:T(8,128)(2,1)}, u32[]{:S(2)}) copy-start(bf16[1024,512]{1,0:T(8,128)(2,1)} %param.17) | copy-start | bytes 3145732
  7.2 314.2 %all-reduce.5.cloned.1.call-start = ((), (), s32[]{:S(2)}) async-start(), calls=%async_computation | async-start | bytes 6291456 | tf_op jit(solution)/shard_map/psum | solution.py:157
  10.1 1.0 copy-start.18
  11.1 33.9 %collective-permute-start = (bf16[3,512]{1,0:T(4,128)(2,1)S(1)}, bf16[3,512]{1,0:T(4,128)(2,1)S(1)}, u32[]{:S(2)}, u32[]{:S(2)}) collective-permute-start(bf16[3,512]{1,0:T(4,128)(2,1)S(1)} %slice.65), channel_id=1, source_target_pairs={{0,4},{4,8},{8,12},{12,0},{1,5},{5,9},{9,13},{13,1},{2,6},{6,10},{... | collective-permute-start | bytes 9224 | tf_op jit(solution)/shard_map/ppermute | solution.py:16
  18.7 5.6 %copy-start.3 = (bf16[2,512,8,64]{1,3,2,0:T(8,128)(2,1)}, bf16[2,512,8,64]{1,3,2,0:T(8,128)(2,1)S(1)}, u32[]{:S(2)}) copy-start(bf16[2,512,8,64]{1,3,2,0:T(8,128)(2,1)S(1)} %copy.51) | copy-start | bytes 3145732
  18.8 5.3 %copy-start.26 = (f32[2,512]{1,0:T(2,128)}, f32[2,512]{1,0:T(2,128)S(1)}, u32[]{:S(2)}) copy-start(f32[2,512]{1,0:T(2,128)S(1)} %multiply_divide_fusion) | copy-start | bytes 12292
  26.5 57.1 %copy-start.14 = (f32[8,64,64]{2,1,0:T(8,128)}, f32[8,64,64]{2,1,0:T(8,128)S(1)}, u32[]{:S(2)}) copy-start(f32[8,64,64]{2,1,0:T(8,128)S(1)} %get-tuple-element.348) | copy-start | bytes 393220
  42.2 5.4 %copy-start.8 = (f32[8,64,64]{2,1,0:T(8,128)}, f32[8,64,64]{2,1,0:T(8,128)S(1)}, u32[]{:S(2)}) copy-start(f32[8,64,64]{2,1,0:T(8,128)S(1)} %get-tuple-element.225) | copy-start | bytes 393220
  42.2 4.1 %copy-start.36 = (bf16[4,512]{1,0:T(4,128)(2,1)S(1)}, bf16[4,512]{1,0:T(4,128)(2,1)}, u32[]{:S(2)}) copy-start(bf16[4,512]{1,0:T(4,128)(2,1)} %param.21) | copy-start | bytes 12292
  45.0 7.6 %collective-permute-start.1 = (bf16[3,512]{1,0:T(4,128)(2,1)S(1)}, bf16[3,512]{1,0:T(4,128)(2,1)S(1)}, u32[]{:S(2)}, u32[]{:S(2)}) collective-permute-start(bf16[3,512]{1,0:T(4,128)(2,1)S(1)} %collective-permute-done), channel_id=1, source_target_pairs={{0,1},{1,2},{2,3},{4,5},{5,6},{6,7},{8,9},{9,10},{10,11},{12,13},{... | collective-permute-start | bytes 9224 | tf_op jit(solution)/shard_map/ppermute | solution.py:22
  46.3 7.8 %copy-start.28 = (f32[1,512]{1,0:T(1,128)}, f32[1,512]{1,0:T(1,128)S(1)}, u32[]{:S(2)}) copy-start(f32[1,512]{1,0:T(1,128)S(1)} %get-tuple-element.342) | copy-start | bytes 6148
  46.3 7.8 %copy-start.30 = (f32[1,512]{1,0:T(1,128)}, f32[1,512]{1,0:T(1,128)S(1)}, u32[]{:S(2)}) copy-start(f32[1,512]{1,0:T(1,128)S(1)} %get-tuple-element.343) | copy-start | bytes 6148
  46.4 7.8 %copy-start.32 = (f32[1,512]{1,0:T(1,128)}, f32[1,512]{1,0:T(1,128)S(1)}, u32[]{:S(2)}) copy-start(f32[1,512]{1,0:T(1,128)S(1)} %get-tuple-element.344) | copy-start | bytes 6148
  46.4 7.8 %copy-start.34 = (f32[1,512]{1,0:T(1,128)}, f32[1,512]{1,0:T(1,128)S(1)}, u32[]{:S(2)}) copy-start(f32[1,512]{1,0:T(1,128)S(1)} %get-tuple-element.345) | copy-start | bytes 6148
  66.1 0.7 copy-start.16
  137.4 3.3 copy-start.7
  137.4 3.3 copy-start.9
  137.4 3.3 copy-start.15
  137.4 3.4 %copy-start.17 = (f32[2,8,64,64]{3,2,1,0:T(8,128)S(1)}, f32[2,8,64,64]{3,2,1,0:T(8,128)}, u32[]{:S(2)}) copy-start(f32[2,8,64,64]{3,2,1,0:T(8,128)} %get-tuple-element.349) | copy-start | bytes 786436
  138.5 3.1 copy-start.27
  141.7 3.0 copy-start.2
  144.7 2.0 copy-start.1
  144.7 2.0 copy-start.4
  144.7 2.5 copy-start.10
  162.2 3.3 copy-start.5
  162.2 3.3 copy-start.6
  171.3 3.0 copy-start.2
  174.3 2.0 copy-start.1
  174.4 2.0 copy-start.4
  174.4 2.5 copy-start.10
  191.8 3.3 copy-start.5
  191.8 3.3 copy-start.6
  201.6 8.3 %collective-permute-start.2 = (bf16[3,512]{1,0:T(4,128)(2,1)S(1)}, bf16[3,512]{1,0:T(4,128)(2,1)S(1)}, u32[]{:S(2)}, u32[]{:S(2)}) collective-permute-start(bf16[3,512]{1,0:T(4,128)(2,1)S(1)} %slice.73), channel_id=1, source_target_pairs={{0,12},{4,0},{8,4},{12,8},{1,13},{5,1},{9,5},{13,9},{2,14},{6,2},{... | collective-permute-start | bytes 9224 | tf_op jit(solution)/shard_map/ppermute | solution.py:16
  206.8 4.3 %copy-start.22 = (bf16[2,512,512]{2,1,0:T(8,128)(2,1)S(1)}, bf16[2,512,512]{2,1,0:T(8,128)(2,1)}, u32[]{:S(2)}) copy-start(bf16[2,512,512]{2,1,0:T(8,128)(2,1)} %get-tuple-element.228) | copy-start | bytes 3145732
  209.8 3.0 collective-permute-start.3
  211.1 1.8 copy-start.11
  212.9 0.6 copy-start.29
  212.9 0.6 copy-start.31
  212.9 0.7 copy-start.33
  212.9 0.7 copy-start.35
  214.5 1.0 copy-start.12
  219.5 35.0 %copy-start.13 = (bf16[1024,512]{1,0:T(8,128)(2,1)S(1)}, bf16[1024,512]{1,0:T(8,128)(2,1)}, u32[]{:S(2)}) copy-start(bf16[1024,512]{1,0:T(8,128)(2,1)} %copy-done.12) | copy-start | bytes 3145732
  219.5 35.0 %copy-start.24 = (bf16[512,512]{1,0:T(8,128)(2,1)S(1)}, bf16[512,512]{1,0:T(8,128)(2,1)}, u32[]{:S(2)}) copy-start(bf16[512,512]{1,0:T(8,128)(2,1)} %param.19) | copy-start | bytes 1572868
  254.5 1.3 copy-start.23
  254.5 1.5 copy-start.25
  321.4 2.7 copy-start.21
  321.4 4.0 %copy-start.20 = (f32[512,512]{0,1:T(8,128)S(1)}, f32[512,512]{0,1:T(8,128)}, u32[]{:S(2)}) copy-start(f32[512,512]{0,1:T(8,128)} %get-tuple-element.337) | copy-start | bytes 3145732
Sparse Core Ops, SparseCore 0:
  217.3 104.0 all-reduce.4
where the time goes:
time: 335 us; the launch traced here: 334 us
  blocking collectives  112 us (33%)
  waiting for transfers between devices  63.8 us (19%)
  matrix products  58.5 us (17%)
  local copies, waits for them, and re-layouts  56.5 us (17%)
  other arithmetic  16.9 us (5%)
  between operations  14.5 us (4%)
  starting transfers between devices  10.8 us (3%)
    psum x1, waiting for transfers between devices, on_device(): lax.psum((local_wq, local_wk, local_wv, conv_local), ('seq', 'outer'))  63.7 us
    all_gather x4, blocking collectives, entering(): gathered = lax.all_gather(x.astype(jnp.bfloat16), axis)  49.7 us
    psum x1, blocking collectives, on_device(): lax.psum((local_wq, local_wk, local_wv, conv_local), ('seq', 'outer'))  32.9 us
    psum x1, blocking collectives, on_device(): kv_group, qdo_group = lax.psum((kv_local, qdo_local), 'seq')  29.6 us
    dynamic_update_slice x10, local copies, waits for them, and re-layouts, on_device(): lax.map(block_grads, (query_heads, key_heads, value_heads, grad_heads, bl...  20.6 us
    unnamed x66, local copies, waits for them, and re-layouts  10.2 us
    dot_general x2, matrix products, block_grads(): jnp.einsum('hts,thj->shj', mixing, grad_rows, preferred_element_type=jnp....  9.25 us
    while x4, local copies, waits for them, and re-layouts, on_device(): lax.map(block_grads, (query_heads, key_heads, value_heads, grad_heads, bl...  9.23 us
  transfers between devices with their start and end apart: 5, of which 1 were waited for; matrix products, arithmetic and copies ran while one was open for 10% of the time, Pallas kernels for 0%

commit v1 on v0

--- a/solution.py
+++ b/solution.py
@@ -155,7 +155,7 @@
     local_wk = lax.dot_general(inputs, grad_pre, over_rows, preferred_element_type=jnp.float32)
     local_wv = lax.dot_general(inputs, grad_value, over_rows, preferred_element_type=jnp.float32)
     grad_wq, grad_wk, grad_wv, grad_conv = lax.psum(
-        (local_wq, local_wk, local_wv, conv_local), ("seq", "outer")
+        lax.psum((local_wq, local_wk, local_wv, conv_local), "outer"), "seq"
     )
     return (grad_inputs, grad_wq, grad_wk, grad_wv, grad_conv)
 

time: 335 us -> 425 us (1.27)
  waiting for transfers between devices: 63.8 us -> 166 us
  blocking collectives: 112 us -> 100 us
    psum x1 -> x2, waiting for transfers between devices: 63.7 us -> 166 us  [the longest x1 97.1 us: on_device(): lax.psum(lax.psum((local_wq, local_wk, local_wv, conv_local), 'outer'), '...]
    psum x1 -> x2, blocking collectives: 32.9 us -> 19.3 us  [the longest x1 13.4 us: on_device(): lax.psum(lax.psum((local_wq, local_wk, local_wv, conv_local), 'outer'), '...]
    unnamed x66 -> x62, local copies, waits for them, and re-layouts: 10.2 us -> 8.59 us
  transfers between devices with their start and end apart: 5 -> 6, of which waited for: 1 -> 2; matrix products, arithmetic and copies ran while one was open for 10% -> 8% of each run, Pallas kernels for 0% -> 0%
where the time goes in v1:
time: 425 us; the launch traced here: 424 us
  waiting for transfers between devices  166 us (39%)
  blocking collectives  100 us (24%)
  matrix products  60.1 us (14%)
  local copies, waits for them, and re-layouts  55 us (13%)
  other arithmetic  16.9 us (4%)
  between operations  14.5 us (3%)
  starting transfers between devices  10.9 us (3%)
    psum x1, waiting for transfers between devices, on_device(): lax.psum(lax.psum((local_wq, local_wk, local_wv, conv_local), 'outer'), '...  97.1 us
    psum x1, waiting for transfers between devices, on_device(): lax.psum((local_wq, local_wk, local_wv, conv_local), 'outer')  68.8 us
    all_gather x4, blocking collectives, entering(): gathered = lax.all_gather(x.astype(jnp.bfloat16), axis)  49.9 us
    psum x1, blocking collectives, on_device(): kv_group, qdo_group = lax.psum((kv_local, qdo_local), 'seq')  30.7 us
    dynamic_update_slice x10, local copies, waits for them, and re-layouts, on_device(): lax.map(block_grads, (query_heads, key_heads, value_heads, grad_heads, bl...  20.7 us
    psum x1, blocking collectives, on_device(): lax.psum(lax.psum((local_wq, local_wk, local_wv, conv_local), 'outer'), '...  13.4 us
    dot_general x2, matrix products, block_grads(): jnp.einsum('hts,thj->shj', mixing, grad_rows, preferred_element_type=jnp....  9.26 us
    while x4, local copies, waits for them, and re-layouts, on_device(): lax.map(block_grads, (query_heads, key_heads, value_heads, grad_heads, bl...  9.25 us
  transfers between devices with their start and end apart: 6, of which 2 were waited for; matrix products, arithmetic and copies ran while one was open for 8% of the time, Pallas kernels for 0%

profile of v1, /device:TPU:0, one launch (start us, length us, event | category | flops | bytes accessed | tf_op | source)
XLA Modules:
  0.0 423.6 jit_solution(4241667613498182519)
XLA Ops:
  8.4 1.7 convolution_convert_fusion.2
  10.2 3.1 collective-permute-start
  13.2 2.1 reshape.136
  15.3 2.5 copy.51
  17.9 2.1 convolution_convert_fusion
  20.0 1.3 copy.47
  21.3 1.8 reshape.123
  23.5 2.1 fusion.64
  25.6 15.2 %all-gather.3 = bf16[32,64,64]{2,1,0:T(8,128)(2,1)S(1)} all-gather(bf16[8,64,64]{2,1,0:T(8,128)(2,1)S(1)} %convert_element_type.173), channel_id=5, replica_groups=mesh['grp'=2,'seq'=4,'outer'=4] {'seq'}, dimensions={0}, use_global_device_ids=true | all-gather | bytes 327680 | tf_op jit(solution)/shard_map/all_gather | solution.py:29
  41.1 2.8 convolution_convert_fusion.1
  46.5 2.8 reshape.137
  49.3 2.2 copy.52
  51.5 1.5 maximum_convert_fusion
  53.1 1.9 add_convert_fusion.1
  55.0 3.9 reshape.135
  58.9 3.3 copy.50
  62.2 2.8 fusion.63
  65.7 17.2 %all-gather.1 = bf16[32,64,64]{2,1,0:T(8,128)(2,1)} all-gather(bf16[8,64,64]{2,1,0:T(8,128)(2,1)S(1)} %convert_element_type.168), channel_id=3, replica_groups=mesh['grp'=2,'seq'=4,'outer'=4] {'seq'}, dimensions={0}, use_global_device_ids=true | all-gather | bytes 327680 | tf_op jit(solution)/shard_map/all_gather | solution.py:29
  82.9 30.7 %all-reduce.10 = (bf16[8,64,64]{2,1,0:T(8,128)(2,1)}, bf16[8,64,64]{2,1,0:T(8,128)(2,1)S(1)}) all-reduce(f32[8,64,64]{2,1,0:T(8,128)} %copy-done.15, f32[8,64,64]{2,1,0:T(8,128)S(1)} %get-tuple-element.351), channel_id=1, replica_groups=mesh['grp'=2,'seq'=4,'outer'=4] {'seq'}, use_global_device_ids=true, to_apply=%region_1.2 | all-reduce | flops 65536 | bytes 393216 | tf_op jit(solution)/shard_map/psum | solution.py:114
  113.6 7.2 %all-gather = bf16[32,64,64]{2,1,0:T(8,128)(2,1)} all-gather(bf16[8,64,64]{2,1,0:T(8,128)(2,1)} %get-tuple-element.338), channel_id=2, replica_groups=mesh['grp'=2,'seq'=4,'outer'=4] {'outer'}, dimensions={0}, use_global_device_ids=true | all-gather | bytes 327680 | tf_op jit(solution)/shard_map/all_gather | solution.py:29
  121.5 10.4 %all-gather.2 = bf16[32,64,64]{2,1,0:T(8,128)(2,1)} all-gather(bf16[8,64,64]{2,1,0:T(8,128)(2,1)S(1)} %get-tuple-element.339), channel_id=4, replica_groups=mesh['grp'=2,'seq'=4,'outer'=4] {'outer'}, dimensions={0}, use_global_device_ids=true | all-gather | bytes 327680 | tf_op jit(solution)/shard_map/all_gather | solution.py:29
  132.7 5.1 %while.60 = (s32[]{:T(128)}, f32[8,64,64]{2,1,0:T(8,128)}, s32[]{:T(128)}, bf16[4,8,64,64]{3,2,1,0:T(8,128)(2,1)}, s32[]{:T(128)}, /*index=5*/s32[]{:T(128)}, s32[]{:T(128)}, s32[]{:T(128)}) while((s32[]{:T(128)}, f32[8,64,64]{2,1,0:T(8,128)}, s32[]{:T(128)}, bf16[4,8,64,64]{3,2,1,0:T(8,128)(2,1)}, s32[]{:T(128)}, /*index=5*/s32[]{:T(128)}, ...), condition=%wide.region_10.11_spmd, body=%wide.region_9.10_spmd.sunk | while | flops 65542 | bytes 327823 | solution.py:36
  132.7 1.7 convert_add_fusion.10
  134.4 1.7 convert_add_fusion.10
  136.1 1.7 convert_add_fusion.10
  138.9 2.2 fusion.61
  142.0 59.3 %while.62 = (s32[]{:T(128)}, bf16[2,512,512]{2,1,0:T(8,128)(2,1)}, bf16[2,512,512]{2,1,0:T(8,128)(2,1)}, bf16[2,512,512]{2,1,0:T(8,128)(2,1)}, bf16[2,512,8,64]{...) while((s32[]{:T(128)}, bf16[2,512,512]{2,1,0:T(8,128)(2,1)}, ...), condition=%wide.region_15.16_spmd, body=%wide.region_14.15_spmd.sunk | while | flops 1960837120 | bytes 65027896 | solution.py:122
  142.1 3.0 select_convert_fusion.6
  145.1 1.4 fusion.128
  147.7 1.4 fusion.129
  149.1 2.1 copy.80
  151.2 1.9 constant_dynamic-update-slice_fusion.5
  153.0 4.6 %fusion.130 = f32[8,64,512]{2,1,0:T(8,128)} fusion(f32[512]{0:T(512)S(1)} %bitcast.174, pred[512,512]{1,0:T(8,128)(4,1)S(1)} %iota_compare_fusion.2, bf16[2,512,8,64]{1,3,2,0:T(8,128)(2,1)} %get-tuple-element.651, s32[]{:T(128)S(6)} %copy.116, bf16[2,512,8,64]{1,3,2,0:T(8,128)(2,1)} %get-tuple-element.647, bf16[2,512,8,64]{1,3,2,0:T(8,128)(2,1)} %get-tuple-element.646), kind=kOutput, calls=%fused_computation.6.clone.1 | convolution fusion | flops 543162368 | bytes 2887168 | tf_op jit(solution)/shard_map/while/body/eval_jaxpr/hts,thj->shj/dot_general | solution.py:62
  157.7 2.9 fusion.131
  160.6 2.1 copy.81
  162.6 3.3 fusion.132
  165.9 1.4 fusion.133
  167.3 2.1 copy.82
  169.4 2.2 constant_dynamic-update-slice_fusion.6
  171.8 3.0 select_convert_fusion.6
  174.8 1.4 fusion.128
  177.3 1.4 fusion.129
  178.7 2.1 copy.80
  180.8 1.9 constant_dynamic-update-slice_fusion.5
  182.7 4.6 %fusion.130 = f32[8,64,512]{2,1,0:T(8,128)} fusion(f32[512]{0:T(512)S(1)} %bitcast.174, pred[512,512]{1,0:T(8,128)(4,1)S(1)} %iota_compare_fusion.2, bf16[2,512,8,64]{1,3,2,0:T(8,128)(2,1)} %get-tuple-element.651, s32[]{:T(128)S(6)} %copy.116, bf16[2,512,8,64]{1,3,2,0:T(8,128)(2,1)} %get-tuple-element.647, bf16[2,512,8,64]{1,3,2,0:T(8,128)(2,1)} %get-tuple-element.646), kind=kOutput, calls=%fused_computation.6.clone.1 | convolution fusion | flops 543162368 | bytes 2887168 | tf_op jit(solution)/shard_map/while/body/eval_jaxpr/hts,thj->shj/dot_general | solution.py:62
  187.3 2.9 fusion.131
  190.2 2.1 copy.81
  192.3 3.3 fusion.132
  195.6 1.4 fusion.133
  197.0 2.1 copy.82
  199.1 2.2 constant_dynamic-update-slice_fusion.6
  202.0 5.2 %collective-permute-start.2 = (bf16[3,512]{1,0:T(4,128)(2,1)S(1)}, bf16[3,512]{1,0:T(4,128)(2,1)S(1)}, u32[]{:S(2)}, u32[]{:S(2)}) collective-permute-start(bf16[3,512]{1,0:T(4,128)(2,1)S(1)} %slice.73), channel_id=1, source_target_pairs={{0,12},{4,0},{8,4},{12,8},{1,13},{5,1},{9,5},{13,9},{2,14},{6,2},{... | collective-permute-start | bytes 9224 | tf_op jit(solution)/shard_map/ppermute | solution.py:16
  207.3 3.0 convolution_bitcast_fusion.2
  211.6 1.7 convolution_bitcast_fusion
  215.9 1.7 convolution_bitcast_fusion.1
  217.7 68.8 %all-reduce.7.cloned.1.call-done = (f32[512,512]{0,1:T(8,128)}, f32[512,512]{0,1:T(8,128)}, f32[512,512]{0,1:T(8,128)}) async-done(((f32[512,512]{0,1:T(8,128)}, f32[512,512]{0,1:T(8,128)}, f32[512,512]{0,1:T(8,128)}), (f32[512,512]{0,1:T(8,128)}, f32[512,512]{0,1:T(8,128)}, f32[512,512]{0,1:T(8,128)})) %all-reduce.7.cloned.1.call-update) | async-done | bytes 3145744 | tf_op jit(solution)/shard_map/psum | solution.py:158
  286.6 2.3 fusion.51
  288.8 5.9 %psum.78 = f32[4,512]{1,0:T(4,128)S(1)} all-reduce(f32[4,512]{1,0:T(4,128)S(1)} %pad_maximum_fusion), channel_id=1, replica_groups=mesh['grp'=2,'seq'=4,'outer'=4] {'outer'}, use_global_device_ids=true, to_apply=%region_26.27 | all-reduce | flops 2048 | bytes 16384 | tf_op jit(solution)/shard_map/psum | solution.py:158
  294.7 13.4 %psum.79 = f32[4,512]{1,0:T(4,128)} all-reduce(f32[4,512]{1,0:T(4,128)S(1)} %psum.78), channel_id=1, replica_groups=mesh['grp'=2,'seq'=4,'outer'=4] {'seq'}, use_global_device_ids=true, to_apply=%region_27.28 | all-reduce | flops 2048 | bytes 16384 | tf_op jit(solution)/shard_map/psum | solution.py:157
  308.2 2.1 fusion.65
  310.3 2.2 fusion.66
  312.5 1.8 add_convert_fusion
  314.3 97.1 %all-reduce.9.cloned.1.call-done = (f32[512,512]{0,1:T(8,128)}, f32[512,512]{0,1:T(8,128)}, f32[512,512]{0,1:T(8,128)}) async-done(((f32[512,512]{0,1:T(8,128)}, f32[512,512]{0,1:T(8,128)}, f32[512,512]{0,1:T(8,128)}), (f32[512,512]{0,1:T(8,128)}, f32[512,512]{0,1:T(8,128)}, f32[512,512]{0,1:T(8,128)})) %all-reduce.9.cloned.1.call-update) | async-done | bytes 3145744 | tf_op jit(solution)/shard_map/psum | solution.py:157
  411.5 2.7 copy.57
  (128 shorter events, 18.5 us)
Async XLA Ops:
  7.2 1.2 copy-start
  7.2 6.1 %copy-start.18 = (bf16[1024,512]{1,0:T(8,128)(2,1)S(1)}, bf16[1024,512]{1,0:T(8,128)(2,1)}, u32[]{:S(2)}) copy-start(bf16[1024,512]{1,0:T(8,128)(2,1)} %param.17) | copy-start | bytes 3145732
  7.2 279.3 %all-reduce.7.cloned.1.call-start = ((), (), s32[]{:S(2)}) async-start(), calls=%async_computation | async-start | bytes 6291456 | tf_op jit(solution)/shard_map/psum | solution.py:158
  10.1 3.1 copy-start.17
  10.2 33.7 %collective-permute-start = (bf16[3,512]{1,0:T(4,128)(2,1)S(1)}, bf16[3,512]{1,0:T(4,128)(2,1)S(1)}, u32[]{:S(2)}, u32[]{:S(2)}) collective-permute-start(bf16[3,512]{1,0:T(4,128)(2,1)S(1)} %slice.65), channel_id=1, source_target_pairs={{0,4},{4,8},{8,12},{12,0},{1,5},{5,9},{9,13},{13,1},{2,6},{6,10},{... | collective-permute-start | bytes 9224 | tf_op jit(solution)/shard_map/ppermute | solution.py:16
  17.8 5.6 %copy-start.3 = (bf16[2,512,8,64]{1,3,2,0:T(8,128)(2,1)}, bf16[2,512,8,64]{1,3,2,0:T(8,128)(2,1)S(1)}, u32[]{:S(2)}) copy-start(bf16[2,512,8,64]{1,3,2,0:T(8,128)(2,1)S(1)} %copy.51) | copy-start | bytes 3145732
  17.9 5.3 %copy-start.24 = (f32[2,512]{1,0:T(2,128)}, f32[2,512]{1,0:T(2,128)S(1)}, u32[]{:S(2)}) copy-start(f32[2,512]{1,0:T(2,128)S(1)} %multiply_divide_fusion) | copy-start | bytes 12292
  25.6 57.3 %copy-start.13 = (f32[8,64,64]{2,1,0:T(8,128)}, f32[8,64,64]{2,1,0:T(8,128)S(1)}, u32[]{:S(2)}) copy-start(f32[8,64,64]{2,1,0:T(8,128)S(1)} %get-tuple-element.351) | copy-start | bytes 393220
  41.0 5.4 %copy-start.8 = (f32[8,64,64]{2,1,0:T(8,128)}, f32[8,64,64]{2,1,0:T(8,128)S(1)}, u32[]{:S(2)}) copy-start(f32[8,64,64]{2,1,0:T(8,128)S(1)} %get-tuple-element.225) | copy-start | bytes 393220
  41.0 4.1 copy-start.34
  43.9 7.6 %collective-permute-start.1 = (bf16[3,512]{1,0:T(4,128)(2,1)S(1)}, bf16[3,512]{1,0:T(4,128)(2,1)S(1)}, u32[]{:S(2)}, u32[]{:S(2)}) collective-permute-start(bf16[3,512]{1,0:T(4,128)(2,1)S(1)} %collective-permute-done), channel_id=1, source_target_pairs={{0,1},{1,2},{2,3},{4,5},{5,6},{6,7},{8,9},{9,10},{10,11},{12,13},{... | collective-permute-start | bytes 9224 | tf_op jit(solution)/shard_map/ppermute | solution.py:22
  45.2 7.9 %copy-start.26 = (f32[1,512]{1,0:T(1,128)}, f32[1,512]{1,0:T(1,128)S(1)}, u32[]{:S(2)}) copy-start(f32[1,512]{1,0:T(1,128)S(1)} %get-tuple-element.345) | copy-start | bytes 6148
  45.2 7.9 %copy-start.28 = (f32[1,512]{1,0:T(1,128)}, f32[1,512]{1,0:T(1,128)S(1)}, u32[]{:S(2)}) copy-start(f32[1,512]{1,0:T(1,128)S(1)} %get-tuple-element.346) | copy-start | bytes 6148
  45.2 7.9 %copy-start.30 = (f32[1,512]{1,0:T(1,128)}, f32[1,512]{1,0:T(1,128)S(1)}, u32[]{:S(2)}) copy-start(f32[1,512]{1,0:T(1,128)S(1)} %get-tuple-element.347) | copy-start | bytes 6148
  45.2 7.9 %copy-start.32 = (f32[1,512]{1,0:T(1,128)}, f32[1,512]{1,0:T(1,128)S(1)}, u32[]{:S(2)}) copy-start(f32[1,512]{1,0:T(1,128)S(1)} %get-tuple-element.348) | copy-start | bytes 6148
  65.0 0.7 copy-start.15
  137.8 3.3 copy-start.7
  137.8 3.3 copy-start.9
  137.8 3.3 copy-start.14
  137.8 3.3 copy-start.16
  138.9 3.1 copy-start.25
  142.1 3.0 copy-start.2
  145.1 2.0 copy-start.1
  145.1 2.0 copy-start.4
  145.1 2.5 copy-start.10
  162.6 3.3 copy-start.5
  162.6 3.3 copy-start.6
  171.8 3.0 copy-start.2
  174.8 2.0 copy-start.1
  174.8 2.0 copy-start.4
  174.8 2.5 copy-start.10
  192.3 3.3 copy-start.5
  192.3 3.3 copy-start.6
  202.0 8.3 %collective-permute-start.2 = (bf16[3,512]{1,0:T(4,128)(2,1)S(1)}, bf16[3,512]{1,0:T(4,128)(2,1)S(1)}, u32[]{:S(2)}, u32[]{:S(2)}) collective-permute-start(bf16[3,512]{1,0:T(4,128)(2,1)S(1)} %slice.73), channel_id=1, source_target_pairs={{0,12},{4,0},{8,4},{12,8},{1,13},{5,1},{9,5},{13,9},{2,14},{6,2},{... | collective-permute-start | bytes 9224 | tf_op jit(solution)/shard_map/ppermute | solution.py:16
  207.3 4.3 %copy-start.21 = (bf16[2,512,512]{2,1,0:T(8,128)(2,1)S(1)}, bf16[2,512,512]{2,1,0:T(8,128)(2,1)}, u32[]{:S(2)}) copy-start(bf16[2,512,512]{2,1,0:T(8,128)(2,1)} %get-tuple-element.228) | copy-start | bytes 3145732
  210.3 3.0 collective-permute-start.3
  211.6 1.8 copy-start.11
  213.3 0.6 copy-start.27
  213.3 0.7 copy-start.29
  213.3 0.7 copy-start.31
  213.3 0.7 copy-start.33
  214.9 1.0 copy-start.12
  217.7 193.8 %all-reduce.9.cloned.1.call-start = ((), (), s32[]{:S(2)}) async-start(), calls=%async_computation.1 | async-start | bytes 6291456 | tf_op jit(solution)/shard_map/psum | solution.py:157
  310.3 2.2 copy-start.22
  310.3 2.2 copy-start.23
  411.5 2.7 copy-start.20
  411.5 4.0 copy-start.19
Sparse Core Ops, SparseCore 0:
  217.8 68.6 all-reduce.6
  289.1 122.3 all-reduce.8
